TPU v7x, 32 devices: a whole 2x2x4 slice. The times are simulated.
32 devices in a mesh: dp: 4 (over z), ctx: 4 (over y, core), tensor: 2 (over x).
Axes of the slice: x: 2, y: 2, z: 4, core: 2. Of those that a mesh axis runs over, the one named last changes fastest.
Arguments:
- hidden_in: bfloat16 [4, 1024, 2048], P('dp', 'ctx'), may hold values from -6 to 6
- attn_norm_gain: float32 [2048], replicated, may hold values from 0.5 to 1.5
- attn_norm_bias: float32 [2048], replicated, may hold values from -2 to 2
- qkv_weight: bfloat16 [2048, 6144], P(None, 'tensor'), may hold values from -0.125 to 0.125
- qkv_bias: float32 [6144], P('tensor'), may hold values from -1.2 to 1.2
- dense_weight: bfloat16 [2048, 2048], P('tensor'), may hold values from -2 to 2
- dense_bias: float32 [2048], replicated, may hold values from -3 to 3
- mlp_norm_gain: float32 [2048], replicated, may hold values from 0.5 to 1.5
- mlp_norm_bias: float32 [2048], replicated, may hold values from -2 to 2
- up_weight: bfloat16 [2048, 8192], P(None, 'tensor'), may hold values from -0.125 to 0.125
- up_bias: float32 [8192], P('tensor'), may hold values from -3 to 3
- down_weight: bfloat16 [8192, 2048], P('tensor'), may hold values from -0.0625 to 0.0625
- down_bias: float32 [2048], replicated, may hold values from -3 to 3
- out_cotangent: bfloat16 [4, 1024, 2048], P('dp', 'ctx'), may hold values from -6 to 6
- subset_ids: int32 [4, 1024], P('dp', 'ctx'), may hold values from 0 to 21
- subset_weights: float32 [22], replicated, may hold values from 0.5 to 2
Outputs:
- layer_out: bfloat16 [4, 1024, 2048], P('dp', 'ctx')
- input_grad: bfloat16 [4, 1024, 2048], P('dp', 'ctx')
- grad_attn_norm_gain: float32 [2048], replicated
- grad_attn_norm_bias: float32 [2048], replicated
- grad_qkv_weight: float32 [2048, 6144], P(('dp', 'ctx'), 'tensor')
- grad_qkv_bias: float32 [6144], P('tensor')
- grad_dense_weight: float32 [2048, 2048], P('tensor', ('dp', 'ctx'))
- grad_dense_bias: float32 [2048], replicated
- grad_mlp_norm_gain: float32 [2048], replicated
- grad_mlp_norm_bias: float32 [2048], replicated
- grad_up_weight: float32 [2048, 8192], P(('dp', 'ctx'), 'tensor')
- grad_up_bias: float32 [8192], P('tensor')
- grad_down_weight: float32 [8192, 2048], P('tensor', ('dp', 'ctx'))
- grad_down_bias: float32 [2048], replicated
Inputs may be any that keep to these rules, and one draw needn't show every extreme that they name: `subset_ids`: the corpus subset of every token, one of 22.
All inputs are finite; a program needn't handle non-finite values.
Results may differ from a plain program's by a relative error of at most 0.012.
Values may be sent and summed in bfloat16 or wider, within the bound.
A program may use at most 256 MiB of HBM per device.

v0:
```python
import math
import jax
import jax.numpy as jnp
from jax import lax
from jax.sharding import PartitionSpec as P

HS = 256
ROT = 64
NORM_EPS = 1e-05


def rope_tables(positions, rot_dims):
    half_dims = rot_dims // 2
    freqs = 10000.0 ** (-(jnp.arange(half_dims, dtype=jnp.float32) * 2.0 / rot_dims))
    angles = positions.astype(jnp.float32)[:, None] * freqs[None, :]
    return (
        jnp.concatenate([jnp.cos(angles), jnp.cos(angles)], -1),
        jnp.concatenate([jnp.sin(angles), jnp.sin(angles)], -1),
    )


def rotate(columns, cosine_table, sine_table):
    half_dims = ROT // 2
    leading = columns[..., :ROT]
    turned = jnp.concatenate([-leading[..., half_dims:], leading[..., :half_dims]], -1)
    moved = leading * cosine_table[:, None, :] + turned * sine_table[:, None, :]
    return jnp.concatenate([moved, columns[..., ROT:]], -1)


def rotate_back(gradient, cosine_table, sine_table):
    half_dims = ROT // 2
    leading = gradient[..., :ROT]
    scaled = leading * sine_table[:, None, :]
    turned = jnp.concatenate([scaled[..., half_dims:], -scaled[..., :half_dims]], -1)
    moved = leading * cosine_table[:, None, :] + turned
    return jnp.concatenate([moved, gradient[..., ROT:]], -1)


def swap(array, axis, bit):
    pairs = [(place, place ^ bit) for place in range(lax.axis_size(axis))]
    return lax.ppermute(array, axis, pairs)


def bits_down(axis):
    size = lax.axis_size(axis)
    return [1 << level for level in reversed(range(size.bit_length() - 1))]


def relative_blocks(array, axis, dim):
    place = lax.axis_index(axis)
    for bit in bits_down(axis):
        size = array.shape[dim]
        halves = array.reshape(
            array.shape[:dim] + (size // (2 * bit), 2, bit) + array.shape[dim + 1 :]
        )
        flipped = jnp.flip(halves, dim + 1)
        array = jnp.where(place & bit != 0, flipped, halves).reshape(array.shape)
    return array


def gather_rows(rows, axis):
    for bit in bits_down(axis):
        rows = jnp.concatenate([rows, swap(rows, axis, bit)], 0)
    return rows


def exchange_rows(rows, axis):
    for bit in bits_down(axis):
        rows = jnp.concatenate([rows[:, :bit], swap(rows[:, bit:], axis, bit)], 0)
    return rows[:, 0]


def block_order(size):
    order = [0]
    bit = size // 2
    while bit:
        order = order + [entry ^ bit for entry in order]
        bit //= 2
    return order


def tensor_sum(part):
    if lax.axis_size("tensor") == 2:
        low = part.astype(jnp.bfloat16)
        return low.astype(jnp.float32) + swap(low, "tensor", 1).astype(jnp.float32)
    return lax.psum(part, "tensor")


def reduce_line(left, right, spec, dim):
    size = lax.axis_size("dp")
    width = left.shape[1] // size
    arrived = None
    bits = [1 << level for level in range(size.bit_length() - 1)]
    count = size
    total = None
    for bit in bits:
        count //= 2
        if total is None:
            send = jnp.einsum(
                spec, left[:, count * width :], right, preferred_element_type=jnp.float32
            )
            keep = jnp.einsum(
                spec, left[:, : count * width], right, preferred_element_type=jnp.float32
            )
        else:
            keep = lax.slice_in_dim(total, 0, count * width, axis=dim)
            send = lax.slice_in_dim(total, count * width, 2 * count * width, axis=dim)
        arrived = swap(send.astype(jnp.bfloat16), "dp", bit)
        total = keep + arrived.astype(jnp.float32)
    return total


def reduce_blocks(total, axis, dim, bits=None):
    size = lax.axis_size(axis)
    for bit in [1 << level for level in range(size.bit_length() - 1)]:
        half = total.shape[dim] // 2
        keep = lax.slice_in_dim(total, 0, half, axis=dim)
        send = lax.slice_in_dim(total, half, 2 * half, axis=dim)
        arrived = swap(send.astype(jnp.bfloat16), axis, bit)
        total = keep + arrived.astype(jnp.float32)
    return total


def spread_columns(rows):
    dp_size, ctx_size = (lax.axis_size("dp"), lax.axis_size("ctx"))
    width = rows.shape[1] // (dp_size * ctx_size)
    blocks = rows.reshape(rows.shape[0], dp_size, ctx_size, width)
    blocks = relative_blocks(relative_blocks(blocks, "dp", 1), "ctx", 2)
    blocks = jnp.stack([blocks[:, entry] for entry in block_order(dp_size)], 2)
    return blocks.reshape(rows.shape[0], ctx_size, dp_size * width)


def local(
    hidden_in,
    attn_norm_gain,
    attn_norm_bias,
    qkv_weight,
    qkv_bias,
    dense_weight,
    dense_bias,
    mlp_norm_gain,
    mlp_norm_bias,
    up_weight,
    up_bias,
    down_weight,
    down_bias,
    out_cotangent,
    subset_ids,
    subset_weights,
):
    seq_count, block_len, model_width = hidden_in.shape
    row_count = seq_count * block_len
    head_count = qkv_weight.shape[1] // (3 * HS)
    ctx_size = lax.axis_size("ctx")
    length = block_len * ctx_size
    score_scale = 1.0 / math.sqrt(HS)
    low_type = jnp.bfloat16
    hidden_rows = hidden_in.reshape(row_count, model_width)
    inputs = hidden_rows.astype(jnp.float32)
    row_mean = jnp.mean(inputs, -1, keepdims=True)
    centered = inputs - row_mean
    inv_std = lax.rsqrt(jnp.mean(centered * centered, -1, keepdims=True) + NORM_EPS)
    normed = centered * inv_std
    attn_in = (normed * attn_norm_gain + attn_norm_bias).astype(low_type)
    mlp_in = (normed * mlp_norm_gain + mlp_norm_bias).astype(low_type)
    subset_count = subset_weights.shape[0]
    matches = subset_ids[..., None] == jnp.arange(subset_count, dtype=jnp.int32)
    row_weight = jnp.sum(jnp.where(matches, subset_weights, 0.0), -1).reshape(row_count, 1)
    grad_out = out_cotangent.reshape(row_count, model_width).astype(jnp.float32) * row_weight
    grad_low = grad_out.astype(low_type)
    grad_out_bias = jnp.sum(grad_out, 0)
    low_part = exchange_rows(spread_columns(grad_low), "ctx")
    hidden_part = exchange_rows(spread_columns(hidden_rows), "ctx").astype(jnp.float32)
    stats = gather_rows(jnp.stack([row_mean[:, 0], inv_std[:, 0]])[None], "ctx")
    mean_all = stats[:, 0].reshape(ctx_size * row_count, 1)
    std_all = stats[:, 1].reshape(ctx_size * row_count, 1)
    normed_part = (hidden_part - mean_all) * std_all

    def own_columns(vector):
        return spread_columns(vector[None])[:, 0]

    mlp_part = (normed_part * own_columns(mlp_norm_gain) + own_columns(mlp_norm_bias)).astype(
        low_type
    )
    attn_part = (normed_part * own_columns(attn_norm_gain) + own_columns(attn_norm_bias)).astype(
        low_type
    )
    hidden_units = up_weight.shape[1]
    pieces = max(1, hidden_units // 1024)
    span = hidden_units // pieces
    down_grads, up_grads, up_bias_parts = ([], [], [])
    branch_part, grad_mlp_in = (None, None)
    for piece in range(pieces):
        cols = slice(piece * span, (piece + 1) * span)
        up_pre = (
            jnp.dot(mlp_in, up_weight[:, cols], preferred_element_type=jnp.float32) + up_bias[cols]
        )
        activated = jax.nn.gelu(up_pre, approximate=False).astype(low_type)
        activated_all = gather_rows(activated, "ctx")
        down_grads.append(reduce_line(low_part, activated_all, "rd,rf->fd", 1))
        grad_act = jnp.einsum(
            "rd,fd->rf", grad_low, down_weight[cols], preferred_element_type=jnp.float32
        )
        gelu_back = jax.vjp(lambda pre_act: jax.nn.gelu(pre_act, approximate=False), up_pre)[1]
        grad_pre = gelu_back(grad_act)[0].astype(low_type)
        grad_pre_all = gather_rows(grad_pre, "ctx")
        up_grads.append(reduce_line(mlp_part, grad_pre_all, "rd,rf->df", 0))
        up_bias_parts.append(jnp.sum(grad_pre.astype(jnp.float32), 0))
        more = jnp.dot(activated, down_weight[cols], preferred_element_type=jnp.float32)
        branch_part = more if branch_part is None else branch_part + more
        more = jnp.einsum(
            "rf,df->rd", grad_pre, up_weight[:, cols], preferred_element_type=jnp.float32
        )
        grad_mlp_in = more if grad_mlp_in is None else grad_mlp_in + more
    qkv_all = jnp.dot(attn_in, qkv_weight, preferred_element_type=jnp.float32) + qkv_bias
    qkv_all = qkv_all.reshape(seq_count, block_len, head_count, 3, HS)
    place = lax.axis_index("ctx")
    steps = jnp.arange(block_len, dtype=jnp.int32)
    positions = place * block_len + steps
    cosine_table, sine_table = rope_tables(positions, ROT)
    query_rows = rotate(qkv_all[:, :, :, 0], cosine_table, sine_table).astype(low_type)
    key_rows = rotate(qkv_all[:, :, :, 1], cosine_table, sine_table).astype(low_type)
    value_rows = qkv_all[:, :, :, 2].astype(low_type)
    pair = jnp.stack([key_rows, value_rows], 0).reshape(2 * seq_count, block_len, head_count * HS)
    whole = gather_rows(jnp.swapaxes(pair, 0, 1), "ctx")
    whole = jnp.swapaxes(whole, 0, 1).reshape(2, seq_count, length, head_count, HS)
    key_whole, value_whole = (whole[0], whole[1])
    key_positions = jnp.concatenate(
        [(place ^ entry) * block_len + steps for entry in block_order(ctx_size)]
    )
    causal = key_positions[None, :] <= positions[:, None]
    raw = jnp.einsum("sqhd,skhd->shqk", query_rows, key_whole, preferred_element_type=jnp.float32)
    scores = jnp.where(causal, raw * score_scale, -1e30)
    row_max = jnp.max(scores, -1, keepdims=True)
    expd = jnp.exp(scores - row_max)
    prob = expd / jnp.sum(expd, -1, keepdims=True)
    prob_low = prob.astype(low_type)
    attn_out = jnp.einsum(
        "shqk,skhd->sqhd", prob_low, value_whole, preferred_element_type=jnp.float32
    ).astype(low_type)
    attn_out = attn_out.reshape(row_count, head_count * HS)
    attn_out_all = gather_rows(attn_out, "ctx")
    grad_dense_weight = reduce_line(low_part, attn_out_all, "rd,rf->fd", 1)
    branch_part = branch_part + jnp.dot(attn_out, dense_weight, preferred_element_type=jnp.float32)
    layer_out = (inputs + tensor_sum(branch_part) + dense_bias + down_bias).astype(low_type)
    layer_out = layer_out.reshape(seq_count, block_len, model_width)
    grad_attn = jnp.einsum("rd,kd->rk", grad_low, dense_weight, preferred_element_type=jnp.float32)
    grad_attn = grad_attn.astype(low_type).reshape(seq_count, block_len, head_count, HS)
    grad_prob = jnp.einsum(
        "sqhd,skhd->shqk", grad_attn, value_whole, preferred_element_type=jnp.float32
    )
    delta = jnp.sum(grad_prob * prob, -1, keepdims=True)
    grad_scores = (prob * (grad_prob - delta)).astype(low_type)
    grad_query = (
        jnp.einsum("shqk,skhd->sqhd", grad_scores, key_whole, preferred_element_type=jnp.float32)
        * score_scale
    )
    grad_key_whole = (
        jnp.einsum("shqk,sqhd->kshd", grad_scores, query_rows, preferred_element_type=jnp.float32)
        * score_scale
    )
    grad_value_whole = jnp.einsum(
        "shqk,sqhd->kshd", prob_low, grad_attn, preferred_element_type=jnp.float32
    )
    grad_pair = jnp.concatenate(
        [
            grad_key_whole.reshape(length, seq_count * head_count * HS),
            grad_value_whole.reshape(length, seq_count * head_count * HS),
        ],
        1,
    )
    grad_pair = reduce_blocks(grad_pair, "ctx", 0)
    grad_pair = grad_pair.reshape(block_len, 2, seq_count, head_count, HS)
    grad_key_rows = jnp.swapaxes(grad_pair[:, 0], 0, 1)
    grad_value_rows = jnp.swapaxes(grad_pair[:, 1], 0, 1)
    grad_qkv = jnp.stack(
        [
            rotate_back(grad_query, cosine_table, sine_table),
            rotate_back(grad_key_rows, cosine_table, sine_table),
            grad_value_rows,
        ],
        3,
    )
    grad_qkv = grad_qkv.reshape(row_count, head_count * 3 * HS).astype(low_type)
    qkv_grads = []
    for head in range(head_count):
        piece = grad_qkv[:, head * 3 * HS : (head + 1) * 3 * HS]
        qkv_grads.append(reduce_line(attn_part, gather_rows(piece, "ctx"), "rd,rc->dc", 0))
    grad_qkv_bias = jnp.sum(grad_qkv.astype(jnp.float32), 0)
    grad_attn_in = jnp.einsum("rc,dc->rd", grad_qkv, qkv_weight, preferred_element_type=jnp.float32)
    norm_parts = jnp.stack(
        [
            jnp.sum(grad_attn_in * normed, 0),
            jnp.sum(grad_attn_in, 0),
            jnp.sum(grad_mlp_in * normed, 0),
            jnp.sum(grad_mlp_in, 0),
        ]
    )
    grad_normed = grad_attn_in * attn_norm_gain + grad_mlp_in * mlp_norm_gain
    input_part = inv_std * (
        grad_normed
        - jnp.mean(grad_normed, -1, keepdims=True)
        - normed * jnp.mean(grad_normed * normed, -1, keepdims=True)
    )
    input_grad = (
        (grad_out + tensor_sum(input_part))
        .astype(low_type)
        .reshape(seq_count, block_len, model_width)
    )
    norm_total = lax.psum(norm_parts, ("dp", "ctx", "tensor"))
    qkv_bias_sum, up_bias_sum, out_bias_sum = lax.psum(
        (grad_qkv_bias, jnp.concatenate(up_bias_parts), grad_out_bias), ("dp", "ctx")
    )
    return (
        layer_out,
        input_grad,
        norm_total[0],
        norm_total[1],
        jnp.concatenate(qkv_grads, 1),
        qkv_bias_sum,
        grad_dense_weight,
        out_bias_sum,
        norm_total[2],
        norm_total[3],
        jnp.concatenate(up_grads, 1),
        up_bias_sum,
        jnp.concatenate(down_grads, 0),
        out_bias_sum,
    )


def solution(mesh):
    return jax.shard_map(
        local,
        mesh=mesh,
        in_specs=(
            P("dp", "ctx", None),
            P(),
            P(),
            P(None, "tensor"),
            P("tensor"),
            P("tensor", None),
            P(),
            P(),
            P(),
            P(None, "tensor"),
            P("tensor"),
            P("tensor", None),
            P(),
            P("dp", "ctx", None),
            P("dp", "ctx"),
            P(),
        ),
        out_specs=(
            P("dp", "ctx", None),
            P("dp", "ctx", None),
            P(),
            P(),
            P(("dp", "ctx"), "tensor"),
            P("tensor"),
            P("tensor", ("dp", "ctx")),
            P(),
            P(),
            P(),
            P(("dp", "ctx"), "tensor"),
            P("tensor"),
            P("tensor", ("dp", "ctx")),
            P(),
        ),
        check_vma=False,
    )
```

profile of v0, /device:TPU:0, one launch (start us, length us, event | category | flops | bytes accessed | tf_op | source)
XLA Modules:
  0.0 691.7 jit_solution(6590537447660785061)
XLA Ops:
  4.1 6.9 multiply_convert_fusion.5
  34.3 9.9 %convolution_add_fusion = f32[256,3072]{1,0:T(8,128)} fusion(bf16[2048,3072]{1,0:T(8,128)(2,1)} %param.19, f32[3072]{0:T(1024)S(1)} %copy-done.93, bf16[1,256,2048]{2,1,0:T(8,128)(2,1)S(1)} %copy-done, f32[2048]{0:T(1024)S(1)} %copy-done.67, f32[2048]{0:T(1024)S(1)} %copy-done.70, f32[256]{0:T(256)S(1)} %add_rsqrt_fusion, f32[256]{0:T(256)S(1)} %broadcast_multiply_fusion.2), kind=kOutput, calls=%fused_computation.12 | convolution fusion | flops 3225157632 | bytes 16807936 | tf_op jit(solution)/shard_map/dot_general | solution.py:215
  85.4 7.3 %convert_reduce_fusion.5 = (f32[1024]{0:T(1024)}, bf16[256,1024]{1,0:T(8,128)(2,1)}) fusion(f32[256,1024]{1,0:T(8,128)S(1)} %copy-done.94, bf16[4096,2048]{1,0:T(8,128)(2,1)} %param.27, bf16[1,256,2048]{2,1,0:T(8,128)(2,1)S(1)} %copy-done.3, f32[256]{0:T(256)S(1)} %fusion.188), kind=kOutput, calls=%fused_computation.202 | convolution fusion | flops 1094712320 | bytes 6820864 | tf_op jit(solution)/shard_map/rd,fd->rf/dot_general | solution.py:201
  158.5 20.1 %collective-permute-done.6 = bf16[256,2,512]{0,2,1:T(8,128)(2,1)S(1)} collective-permute-done((bf16[256,2,512]{0,2,1:T(8,128)(2,1)S(1)}, bf16[256,2,512]{0,2,1:T(8,128)(2,1)S(1)}, u32[]{:S(2)}, u32[]{:S(2)}) %collective-permute-start.6) | collective-permute-done | bytes 524320 | tf_op jit(solution)/shard_map/ppermute | solution.py:41
  178.7 11.0 %collective-permute-done.28 = bf16[256,2,512]{0,2,1:T(8,128)(2,1)S(1)} collective-permute-done((bf16[256,2,512]{0,2,1:T(8,128)(2,1)S(1)}, bf16[256,2,512]{0,2,1:T(8,128)(2,1)S(1)}, u32[]{:S(2)}, u32[]{:S(2)}) %collective-permute-start.28) | collective-permute-done | bytes 524320 | tf_op jit(solution)/shard_map/ppermute | solution.py:41
  191.4 9.6 %collective-permute-done.40 = bf16[256,1024]{1,0:T(8,128)(2,1)S(1)} collective-permute-done((bf16[256,1024]{1,0:T(8,128)(2,1)}, bf16[256,1024]{1,0:T(8,128)(2,1)S(1)}, u32[]{:S(2)}, u32[]{:S(2)}) %collective-permute-start.40) | collective-permute-done | bytes 524320 | tf_op jit(solution)/shard_map/ppermute | solution.py:41
  203.3 31.0 %collective-permute-done.44 = bf16[256,1024]{1,0:T(8,128)(2,1)S(1)} collective-permute-done((bf16[256,1024]{1,0:T(8,128)(2,1)S(1)}, bf16[256,1024]{1,0:T(8,128)(2,1)S(1)}, u32[]{:S(2)}, u32[]{:S(2)}) %collective-permute-start.44) | collective-permute-done | bytes 524320 | tf_op jit(solution)/shard_map/ppermute | solution.py:41
  270.6 7.4 %collective-permute-done.54 = bf16[1024,256]{1,0:T(8,128)(2,1)S(1)} collective-permute-done((bf16[1024,256]{1,0:T(8,128)(2,1)S(1)}, bf16[1024,256]{1,0:T(8,128)(2,1)S(1)}, u32[]{:S(2)}, u32[]{:S(2)}) %collective-permute-start.54) | collective-permute-done | bytes 524320 | tf_op jit(solution)/shard_map/ppermute | solution.py:41
  281.8 7.4 %collective-permute-done.58 = bf16[1024,256]{1,0:T(8,128)(2,1)S(1)} collective-permute-done((bf16[1024,256]{1,0:T(8,128)(2,1)S(1)}, bf16[1024,256]{1,0:T(8,128)(2,1)S(1)}, u32[]{:S(2)}, u32[]{:S(2)}) %collective-permute-start.58) | collective-permute-done | bytes 524320 | tf_op jit(solution)/shard_map/ppermute | solution.py:41
  293.2 7.3 %collective-permute-done.62 = bf16[1024,256]{1,0:T(8,128)(2,1)S(1)} collective-permute-done((bf16[1024,256]{1,0:T(8,128)(2,1)S(1)}, bf16[1024,256]{1,0:T(8,128)(2,1)S(1)}, u32[]{:S(2)}, u32[]{:S(2)}) %collective-permute-start.62) | collective-permute-done | bytes 524320 | tf_op jit(solution)/shard_map/ppermute | solution.py:41
  304.0 7.7 %collective-permute-done.34 = bf16[256,1024]{1,0:T(8,128)(2,1)S(1)} collective-permute-done((bf16[256,1024]{1,0:T(8,128)(2,1)S(1)}, bf16[256,1024]{1,0:T(8,128)(2,1)S(1)}, u32[]{:S(2)}, u32[]{:S(2)}) %collective-permute-start.34) | collective-permute-done | bytes 524320 | tf_op jit(solution)/shard_map/ppermute | solution.py:41
  316.3 12.3 %collective-permute-done.38 = bf16[256,1024]{1,0:T(8,128)(2,1)S(1)} collective-permute-done((bf16[256,1024]{1,0:T(8,128)(2,1)S(1)}, bf16[256,1024]{1,0:T(8,128)(2,1)S(1)}, u32[]{:S(2)}, u32[]{:S(2)}) %collective-permute-start.38) | collective-permute-done | bytes 524320 | tf_op jit(solution)/shard_map/ppermute | solution.py:41
  332.3 13.1 %collective-permute-done.42 = bf16[256,1024]{1,0:T(8,128)(2,1)S(1)} collective-permute-done((bf16[256,1024]{1,0:T(8,128)(2,1)S(1)}, bf16[256,1024]{1,0:T(8,128)(2,1)S(1)}, u32[]{:S(2)}, u32[]{:S(2)}) %collective-permute-start.42) | collective-permute-done | bytes 524320 | tf_op jit(solution)/shard_map/ppermute | solution.py:41
  348.9 7.1 %collective-permute-done.46 = bf16[256,1024]{1,0:T(8,128)(2,1)S(1)} collective-permute-done((bf16[256,1024]{1,0:T(8,128)(2,1)S(1)}, bf16[256,1024]{1,0:T(8,128)(2,1)S(1)}, u32[]{:S(2)}, u32[]{:S(2)}) %collective-permute-start.46) | collective-permute-done | bytes 524320 | tf_op jit(solution)/shard_map/ppermute | solution.py:41
  364.0 21.9 %collective-permute-done.59 = bf16[1024,128]{1,0:T(8,128)(2,1)S(1)} collective-permute-done((bf16[1024,128]{1,0:T(8,128)(2,1)S(1)}, bf16[1024,128]{1,0:T(8,128)(2,1)S(1)}, u32[]{:S(2)}, u32[]{:S(2)}) %collective-permute-start.59) | collective-permute-done | bytes 262176 | tf_op jit(solution)/shard_map/ppermute | solution.py:41
  386.0 11.2 %collective-permute-done.63 = bf16[1024,128]{1,0:T(8,128)(2,1)S(1)} collective-permute-done((bf16[1024,128]{1,0:T(8,128)(2,1)S(1)}, bf16[1024,128]{1,0:T(8,128)(2,1)S(1)}, u32[]{:S(2)}, u32[]{:S(2)}) %collective-permute-start.63) | collective-permute-done | bytes 262176 | tf_op jit(solution)/shard_map/ppermute | solution.py:41
  397.2 11.2 %collective-permute-done.35 = bf16[128,1024]{1,0:T(8,128)(2,1)S(1)} collective-permute-done((bf16[128,1024]{1,0:T(8,128)(2,1)S(1)}, bf16[128,1024]{1,0:T(8,128)(2,1)S(1)}, u32[]{:S(2)}, u32[]{:S(2)}) %collective-permute-start.35) | collective-permute-done | bytes 262176 | tf_op jit(solution)/shard_map/ppermute | solution.py:41
  420.8 8.5 %collective-permute-done.26 = bf16[256,1024]{0,1:T(8,128)(2,1)S(1)} collective-permute-done((bf16[256,1024]{0,1:T(8,128)(2,1)S(1)}, bf16[256,1024]{0,1:T(8,128)(2,1)S(1)}, u32[]{:S(2)}, u32[]{:S(2)}) %collective-permute-start.26) | collective-permute-done | bytes 524320 | tf_op jit(solution)/shard_map/ppermute | solution.py:41
  451.6 12.3 %collective-permute-done.31 = bf16[1024,128]{1,0:T(8,128)(2,1)S(1)} collective-permute-done((bf16[1024,128]{1,0:T(8,128)(2,1)S(1)}, bf16[1024,128]{1,0:T(8,128)(2,1)S(1)}, u32[]{:S(2)}, u32[]{:S(2)}) %collective-permute-start.31) | collective-permute-done | bytes 262176 | tf_op jit(solution)/shard_map/ppermute | solution.py:41
  478.2 9.7 %fusion.236 = (f32[256]{0:T(256)S(1)}, f32[256]{0:T(256)S(1)}, f32[2048]{0:T(1024)S(1)}, f32[2048]{0:T(1024)S(1)}, f32[2048]{0:T(1024)S(1)}, /*index=5*/f32[2048]{0:T(1024)S(1)}, f32[256,2048]{1,0:T(8,128)S(1)}) fusion(f32[256]{0:T(256)S(1)} %copy-done.62, f32[256]{0:T(256)S(1)} %copy-done.54, bf16[1,256,2048]{2,1,0:T(8,128)(2,1)S(1)} %copy-done.1, ...), kind=kOutput, calls=%fused_computation.457 | convolution fusion | flops 3229081088 | bytes 19451904 | tf_op jit(solution)/shard_map/rc,dc->rd/dot_general | solution.py:290
  498.3 59.7 %psum.28 = f32[4,2048]{1,0:T(4,128)S(1)} all-reduce(f32[4,2048]{1,0:T(4,128)S(1)} %pad_maximum_fusion.68), channel_id=1, replica_groups=mesh['dp'=4,'ctx'=4,'tensor'=2] {'dp','ctx','tensor'}, use_global_device_ids=true, to_apply=%region_12.13 | all-reduce | flops 8192 | bytes 65536 | tf_op jit(solution)/shard_map/psum | solution.py:310
  568.9 61.6 %all-reduce = (f32[3072]{0:T(1024)}, f32[2048]{0:T(1024)S(1)}, f32[4096]{0:T(1024)}) all-reduce(f32[3072]{0:T(1024)S(1)} %reduce_sum.167, f32[2048]{0:T(1024)S(1)} %get-tuple-element.40, f32[4096]{0:T(1024)S(1)} %pad_maximum_fusion.69), channel_id=1, replica_groups=mesh['dp'=4,'ctx'=4,'tensor'=2] {'dp','ctx'}, use_global_device_ids=true, to_apply=%region_14.15 | all-reduce | flops 9216 | bytes 73728 | tf_op jit(solution)/shard_map/psum | solution.py:311
  648.9 10.6 %collective-permute-done.16 = bf16[256,768]{1,0:T(8,128)(2,1)S(1)} collective-permute-done((bf16[256,768]{1,0:T(8,128)(2,1)S(1)}, bf16[256,768]{1,0:T(8,128)(2,1)S(1)}, u32[]{:S(2)}, u32[]{:S(2)}) %collective-permute-start.16) | collective-permute-done | bytes 393248 | tf_op jit(solution)/shard_map/ppermute | solution.py:41
  673.4 9.9 %collective-permute-done.17 = bf16[128,768]{1,0:T(8,128)(2,1)S(1)} collective-permute-done((bf16[128,768]{1,0:T(8,128)(2,1)S(1)}, bf16[128,768]{1,0:T(8,128)(2,1)S(1)}, u32[]{:S(2)}, u32[]{:S(2)}) %collective-permute-start.17) | collective-permute-done | bytes 196640 | tf_op jit(solution)/shard_map/ppermute | solution.py:41
  (545 shorter events, 314.0 us)
Async XLA Ops:
  11.1 131.1 %collective-permute-start.48 = (bf16[256,1024]{1,0:T(8,128)(2,1)}, bf16[256,1024]{1,0:T(8,128)(2,1)}, u32[]{:S(2)}, u32[]{:S(2)}) collective-permute-start(bf16[256,1024]{1,0:T(8,128)(2,1)} %get-tuple-element.108), channel_id=1, source_target_pairs={{0,4},{2,6},{4,0},{6,2},{1,5},{3,7},{5,1},{7,3},{8,12},{10,14},{12... | collective-permute-start | bytes 1572872 | tf_op jit(solution)/shard_map/ppermute | solution.py:41
  18.7 127.8 %collective-permute-start.52 = (bf16[256,1024]{1,0:T(8,128)(2,1)}, bf16[256,1024]{1,0:T(8,128)(2,1)}, u32[]{:S(2)}, u32[]{:S(2)}) collective-permute-start(bf16[256,1024]{1,0:T(8,128)(2,1)} %get-tuple-element.106), channel_id=1, source_target_pairs={{0,4},{2,6},{4,0},{6,2},{1,5},{3,7},{5,1},{7,3},{8,12},{10,14},{12... | collective-permute-start | bytes 1572872 | tf_op jit(solution)/shard_map/ppermute | solution.py:41
  23.3 125.5 %collective-permute-start.56 = (bf16[256,1024]{1,0:T(8,128)(2,1)}, bf16[256,1024]{1,0:T(8,128)(2,1)}, u32[]{:S(2)}, u32[]{:S(2)}) collective-permute-start(bf16[256,1024]{1,0:T(8,128)(2,1)} %get-tuple-element.110), channel_id=1, source_target_pairs={{0,4},{2,6},{4,0},{6,2},{1,5},{3,7},{5,1},{7,3},{8,12},{10,14},{12... | collective-permute-start | bytes 1572872 | tf_op jit(solution)/shard_map/ppermute | solution.py:41
  30.1 123.0 %collective-permute-start.60 = (bf16[256,1024]{1,0:T(8,128)(2,1)}, bf16[256,1024]{1,0:T(8,128)(2,1)}, u32[]{:S(2)}, u32[]{:S(2)}) collective-permute-start(bf16[256,1024]{1,0:T(8,128)(2,1)} %get-tuple-element.112), channel_id=1, source_target_pairs={{0,4},{2,6},{4,0},{6,2},{1,5},{3,7},{5,1},{7,3},{8,12},{10,14},{12... | collective-permute-start | bytes 1572872 | tf_op jit(solution)/shard_map/ppermute | solution.py:41
  30.7 107.6 %collective-permute-start.8 = (f32[1,2,256]{2,1,0:T(2,128)}, f32[1,2,256]{2,1,0:T(2,128)}, u32[]{:S(2)}, u32[]{:S(2)}) collective-permute-start(f32[1,2,256]{2,1,0:T(2,128)} %maximum_bitcast_fusion.9), channel_id=1, source_target_pairs={{0,4},{2,6},{4,0},{6,2},{1,5},{3,7},{5,1},{7,3},{8,12},{10,14},{12... | collective-permute-start | bytes 6152 | tf_op jit(solution)/shard_map/ppermute | solution.py:41
  156.0 81.7 %collective-permute-start = (bf16[256,2,1024]{0,2,1:T(8,128)(2,1)S(1)}, bf16[256,2,1024]{0,2,1:T(8,128)(2,1)S(1)}, u32[]{:S(2)}, u32[]{:S(2)}) collective-permute-start(bf16[256,2,1024]{0,2,1:T(8,128)(2,1)S(1)} %maximum_bitcast_fusion.1), channel_id=1, source_target_pairs={{0,4},{2,6},{4,0},{6,2},{1,5},{3,7},{5,1},{7,3},{8,12},{10,14},{12... | collective-permute-start | bytes 3145736 | tf_op jit(solution)/shard_map/ppermute | solution.py:41
  178.5 55.8 %collective-permute-start.44 = (bf16[256,1024]{1,0:T(8,128)(2,1)S(1)}, bf16[256,1024]{1,0:T(8,128)(2,1)S(1)}, u32[]{:S(2)}, u32[]{:S(2)}) collective-permute-start(bf16[256,1024]{1,0:T(8,128)(2,1)S(1)} %get-tuple-element.115), channel_id=1, source_target_pairs={{0,4},{2,6},{4,0},{6,2},{1,5},{3,7},{5,1},{7,3},{8,12},{10,14},{12... | collective-permute-start | bytes 1572872 | tf_op jit(solution)/shard_map/ppermute | solution.py:41
  189.7 51.6 %collective-permute-start.49 = (bf16[512,1024]{1,0:T(8,128)(2,1)}, bf16[512,1024]{1,0:T(8,128)(2,1)}, u32[]{:S(2)}, u32[]{:S(2)}) collective-permute-start(bf16[512,1024]{1,0:T(8,128)(2,1)} %pad_maximum_fusion.26), channel_id=1, source_target_pairs={{0,2},{2,0},{4,6},{6,4},{1,3},{3,1},{5,7},{7,5},{8,10},{10,8},{12,... | collective-permute-start | bytes 3145736 | tf_op jit(solution)/shard_map/ppermute | solution.py:41
  249.4 159.1 %collective-permute-start.1 = (bf16[512,2,1024]{0,2,1:T(8,128)(2,1)S(1)}, bf16[512,2,1024]{0,2,1:T(8,128)(2,1)S(1)}, u32[]{:S(2)}, u32[]{:S(2)}) collective-permute-start(bf16[512,2,1024]{0,2,1:T(8,128)(2,1)S(1)} %copy-done.12), channel_id=1, source_target_pairs={{0,2},{2,0},{4,6},{6,4},{1,3},{3,1},{5,7},{7,5},{8,10},{10,8},{12,... | collective-permute-start | bytes 6291464 | tf_op jit(solution)/shard_map/ppermute | solution.py:41
  278.0 50.6 %collective-permute-start.38 = (bf16[256,1024]{1,0:T(8,128)(2,1)S(1)}, bf16[256,1024]{1,0:T(8,128)(2,1)S(1)}, u32[]{:S(2)}, u32[]{:S(2)}) collective-permute-start(bf16[256,1024]{1,0:T(8,128)(2,1)S(1)} %convolution_convert_fusion.6), channel_id=1, source_target_pairs={{0,8},{8,0},{16,24},{24,16},{1,9},{9,1},{17,25},{25,17},{2,10},{10... | collective-permute-start | bytes 1572872 | tf_op jit(solution)/shard_map/ppermute | solution.py:41
  289.2 56.2 %collective-permute-start.42 = (bf16[256,1024]{1,0:T(8,128)(2,1)S(1)}, bf16[256,1024]{1,0:T(8,128)(2,1)S(1)}, u32[]{:S(2)}, u32[]{:S(2)}) collective-permute-start(bf16[256,1024]{1,0:T(8,128)(2,1)S(1)} %convolution_convert_fusion.5), channel_id=1, source_target_pairs={{0,8},{8,0},{16,24},{24,16},{1,9},{9,1},{17,25},{25,17},{2,10},{10... | collective-permute-start | bytes 1572872 | tf_op jit(solution)/shard_map/ppermute | solution.py:41
  300.5 55.5 %collective-permute-start.46 = (bf16[256,1024]{1,0:T(8,128)(2,1)S(1)}, bf16[256,1024]{1,0:T(8,128)(2,1)S(1)}, u32[]{:S(2)}, u32[]{:S(2)}) collective-permute-start(bf16[256,1024]{1,0:T(8,128)(2,1)S(1)} %convolution_convert_fusion.4), channel_id=1, source_target_pairs={{0,8},{8,0},{16,24},{24,16},{1,9},{9,1},{17,25},{25,17},{2,10},{10... | collective-permute-start | bytes 1572872 | tf_op jit(solution)/shard_map/ppermute | solution.py:41
  311.7 48.8 %collective-permute-start.51 = (bf16[1024,128]{1,0:T(8,128)(2,1)S(1)}, bf16[1024,128]{1,0:T(8,128)(2,1)S(1)}, u32[]{:S(2)}, u32[]{:S(2)}) collective-permute-start(bf16[1024,128]{1,0:T(8,128)(2,1)S(1)} %slice.843), channel_id=1, source_target_pairs={{0,16},{8,24},{16,0},{24,8},{1,17},{9,25},{17,1},{25,9},{2,18},{10... | collective-permute-start | bytes 786440 | tf_op jit(solution)/shard_map/ppermute | solution.py:41
  362.3 56.0 %collective-permute-start.39 = (bf16[128,1024]{1,0:T(8,128)(2,1)}, bf16[128,1024]{1,0:T(8,128)(2,1)}, u32[]{:S(2)}, u32[]{:S(2)}) collective-permute-start(bf16[128,1024]{1,0:T(8,128)(2,1)} %slice.846), channel_id=1, source_target_pairs={{0,16},{8,24},{16,0},{24,8},{1,17},{9,25},{17,1},{25,9},{2,18},{10... | collective-permute-start | bytes 786440 | tf_op jit(solution)/shard_map/ppermute | solution.py:41
  441.1 48.3 %collective-permute-start.2 = (bf16[256,2048]{1,0:T(8,128)(2,1)}, bf16[256,2048]{1,0:T(8,128)(2,1)}, u32[]{:S(2)}, u32[]{:S(2)}) collective-permute-start(bf16[256,2048]{1,0:T(8,128)(2,1)} %fusion.57), channel_id=1, source_target_pairs={{0,1},{1,0},{2,3},{3,2},{4,5},{5,4},{6,7},{7,6},{8,9},{9,8},{10,11... | collective-permute-start | bytes 3145736 | tf_op jit(solution)/shard_map/ppermute | solution.py:41
  489.0 69.0 %collective-permute-start.10 = (bf16[256,768]{0,1:T(8,128)(2,1)}, bf16[256,768]{0,1:T(8,128)(2,1)}, u32[]{:S(2)}, u32[]{:S(2)}) collective-permute-start(bf16[256,768]{0,1:T(8,128)(2,1)} %get-tuple-element.34), channel_id=1, source_target_pairs={{0,4},{2,6},{4,0},{6,2},{1,5},{3,7},{5,1},{7,3},{8,12},{10,14},{12... | collective-permute-start | bytes 1179656 | tf_op jit(solution)/shard_map/ppermute | solution.py:41
  493.1 72.9 %collective-permute-start.5 = (bf16[256,2048]{1,0:T(8,128)(2,1)S(1)}, bf16[256,2048]{1,0:T(8,128)(2,1)}, u32[]{:S(2)}, u32[]{:S(2)}) collective-permute-start(bf16[256,2048]{1,0:T(8,128)(2,1)S(1)} %get-tuple-element.58), channel_id=1, source_target_pairs={{0,1},{1,0},{2,3},{3,2},{4,5},{5,4},{6,7},{7,6},{8,9},{9,8},{10,11... | collective-permute-start | bytes 3145736 | tf_op jit(solution)/shard_map/ppermute | solution.py:41
  494.7 66.1 %collective-permute-start.14 = (bf16[256,768]{0,1:T(8,128)(2,1)}, bf16[256,768]{0,1:T(8,128)(2,1)S(1)}, u32[]{:S(2)}, u32[]{:S(2)}) collective-permute-start(bf16[256,768]{0,1:T(8,128)(2,1)} %get-tuple-element.37), channel_id=1, source_target_pairs={{0,4},{2,6},{4,0},{6,2},{1,5},{3,7},{5,1},{7,3},{8,12},{10,14},{12... | collective-permute-start | bytes 1179656 | tf_op jit(solution)/shard_map/ppermute | solution.py:41
  496.2 67.3 %collective-permute-start.18 = (bf16[256,768]{0,1:T(8,128)(2,1)S(1)}, bf16[256,768]{0,1:T(8,128)(2,1)S(1)}, u32[]{:S(2)}, u32[]{:S(2)}) collective-permute-start(bf16[256,768]{0,1:T(8,128)(2,1)S(1)} %get-tuple-element.36), channel_id=1, source_target_pairs={{0,4},{2,6},{4,0},{6,2},{1,5},{3,7},{5,1},{7,3},{8,12},{10,14},{12... | collective-permute-start | bytes 1179656 | tf_op jit(solution)/shard_map/ppermute | solution.py:41
  496.7 67.8 %collective-permute-start.22 = (bf16[256,768]{0,1:T(8,128)(2,1)S(1)}, bf16[256,768]{0,1:T(8,128)(2,1)S(1)}, u32[]{:S(2)}, u32[]{:S(2)}) collective-permute-start(bf16[256,768]{0,1:T(8,128)(2,1)S(1)} %get-tuple-element.35), channel_id=1, source_target_pairs={{0,4},{2,6},{4,0},{6,2},{1,5},{3,7},{5,1},{7,3},{8,12},{10,14},{12... | collective-permute-start | bytes 1179656 | tf_op jit(solution)/shard_map/ppermute | solution.py:41
  560.1 70.4 %collective-permute-start.11 = (bf16[512,768]{0,1:T(8,128)(2,1)}, bf16[512,768]{0,1:T(8,128)(2,1)}, u32[]{:S(2)}, u32[]{:S(2)}) collective-permute-start(bf16[512,768]{0,1:T(8,128)(2,1)} %pad_maximum_fusion.48), channel_id=1, source_target_pairs={{0,2},{2,0},{4,6},{6,4},{1,3},{3,1},{5,7},{7,5},{8,10},{10,8},{12,... | collective-permute-start | bytes 2359304 | tf_op jit(solution)/shard_map/ppermute | solution.py:41
  562.9 69.7 %collective-permute-start.15 = (bf16[512,768]{0,1:T(8,128)(2,1)}, bf16[512,768]{0,1:T(8,128)(2,1)}, u32[]{:S(2)}, u32[]{:S(2)}) collective-permute-start(bf16[512,768]{0,1:T(8,128)(2,1)} %pad_maximum_fusion.49), channel_id=1, source_target_pairs={{0,2},{2,0},{4,6},{6,4},{1,3},{3,1},{5,7},{7,5},{8,10},{10,8},{12,... | collective-permute-start | bytes 2359304 | tf_op jit(solution)/shard_map/ppermute | solution.py:41
  564.5 72.1 %collective-permute-start.19 = (bf16[512,768]{0,1:T(8,128)(2,1)}, bf16[512,768]{0,1:T(8,128)(2,1)}, u32[]{:S(2)}, u32[]{:S(2)}) collective-permute-start(bf16[512,768]{0,1:T(8,128)(2,1)} %pad_maximum_fusion.50), channel_id=1, source_target_pairs={{0,2},{2,0},{4,6},{6,4},{1,3},{3,1},{5,7},{7,5},{8,10},{10,8},{12,... | collective-permute-start | bytes 2359304 | tf_op jit(solution)/shard_map/ppermute | solution.py:41
  565.5 73.0 %collective-permute-start.23 = (bf16[512,768]{0,1:T(8,128)(2,1)}, bf16[512,768]{0,1:T(8,128)(2,1)}, u32[]{:S(2)}, u32[]{:S(2)}) collective-permute-start(bf16[512,768]{0,1:T(8,128)(2,1)} %pad_maximum_fusion.51), channel_id=1, source_target_pairs={{0,2},{2,0},{4,6},{6,4},{1,3},{3,1},{5,7},{7,5},{8,10},{10,8},{12,... | collective-permute-start | bytes 2359304 | tf_op jit(solution)/shard_map/ppermute | solution.py:41
  (154 other events, 2057.0 us)
where the time goes:
time: 702 us; the launch traced here: 692 us
  waiting for transfers between devices  248 us (35%)
  matrix products  147 us (21%)
  blocking collectives  121 us (17%)
  other arithmetic  74.1 us (11%)
  starting transfers between devices  51.7 us (7%)
  local copies, waits for them, and re-layouts  46.3 us (7%)
    ppermute x64, waiting for transfers between devices, swap(): return lax.ppermute(array, axis, pairs)  248 us
    psum x1, blocking collectives, local(): lax.psum((grad_qkv_bias, jnp.concatenate(up_bias_parts), grad_out_bias),...  61.6 us
    psum x1, blocking collectives, local(): norm_total = lax.psum(norm_parts, ('dp', 'ctx', 'tensor'))  59.7 us
    ppermute x64, starting transfers between devices, swap(): return lax.ppermute(array, axis, pairs)  51.7 us
    concatenate x16, other arithmetic, gather_rows(): rows = jnp.concatenate([rows, swap(rows, axis, bit)], 0)  24.4 us
    dot_general x13, matrix products, reduce_line(): jnp.einsum(spec, left[:, count * width:], right, preferred_element_type=j...  24 us
    dot_general x13, matrix products, reduce_line(): jnp.einsum(spec, left[:, :count * width], right, preferred_element_type=j...  23.1 us
    dot_general x4, matrix products, local(): jnp.einsum('rd,fd->rf', grad_low, down_weight[cols], preferred_element_ty...  21.9 us
  transfers between devices with their start and end apart: 64, of which 27 were waited for; matrix products, arithmetic and copies ran while one was open for 36% of the time, Pallas kernels for 0%

commit v1 on v0

--- a/solution.py
+++ b/solution.py
@@ -308,8 +308,14 @@
         .reshape(seq_count, block_len, model_width)
     )
     norm_total = lax.psum(norm_parts, ("dp", "ctx", "tensor"))
-    qkv_bias_sum, up_bias_sum, out_bias_sum = lax.psum(
-        (grad_qkv_bias, jnp.concatenate(up_bias_parts), grad_out_bias), ("dp", "ctx")
+
+    def update_the_column(a0, device_axis, which_axis="dp"):
+        for j in (device_axis, which_axis):
+            a0 = lax.psum(a0, j)
+        return a0
+
+    qkv_bias_sum, up_bias_sum, out_bias_sum = update_the_column(
+        (grad_qkv_bias, jnp.concatenate(up_bias_parts), grad_out_bias), "ctx"
     )
     return (
         layer_out,

time: 702 us -> 670 us (0.954)
  blocking collectives: 121 us -> 91.2 us
    psum x1 -> x2, blocking collectives: 61.6 us -> 31.5 us  [update_the_column(): a0 = lax.psum(a0, j)]
  transfers between devices with their start and end apart: 64 -> 64, of which waited for: 27 -> 27; matrix products, arithmetic and copies ran while one was open for 36% -> 38% of each run, Pallas kernels for 0% -> 0%
where the time goes in v1:
time: 670 us; the launch traced here: 660 us
  waiting for transfers between devices  246 us (37%)
  matrix products  147 us (22%)
  blocking collectives  91.2 us (14%)
  other arithmetic  74.1 us (11%)
  starting transfers between devices  51.3 us (8%)
  local copies, waits for them, and re-layouts  46.3 us (7%)
    ppermute x64, waiting for transfers between devices, swap(): return lax.ppermute(array, axis, pairs)  246 us
    psum x1, blocking collectives, local(): norm_total = lax.psum(norm_parts, ('dp', 'ctx', 'tensor'))  59.7 us
    ppermute x64, starting transfers between devices, swap(): return lax.ppermute(array, axis, pairs)  51.3 us
    psum x2, blocking collectives, update_the_column(): a0 = lax.psum(a0, j)  31.5 us
    concatenate x16, other arithmetic, gather_rows(): rows = jnp.concatenate([rows, swap(rows, axis, bit)], 0)  24.5 us
    dot_general x13, matrix products, reduce_line(): jnp.einsum(spec, left[:, count * width:], right, preferred_element_type=j...  24 us
    dot_general x13, matrix products, reduce_line(): jnp.einsum(spec, left[:, :count * width], right, preferred_element_type=j...  23.2 us
    dot_general x4, matrix products, local(): jnp.einsum('rd,fd->rf', grad_low, down_weight[cols], preferred_element_ty...  21.9 us
  transfers between devices with their start and end apart: 64, of which 27 were waited for; matrix products, arithmetic and copies ran while one was open for 38% of the time, Pallas kernels for 0%

profile of v1, /device:TPU:0, one launch (start us, length us, event | category | flops | bytes accessed | tf_op | source)
XLA Modules:
  0.0 659.5 jit_solution(12211364025811393410)
XLA Ops:
  34.3 9.9 %convolution_add_fusion = f32[256,3072]{1,0:T(8,128)} fusion(bf16[2048,3072]{1,0:T(8,128)(2,1)} %param.19, f32[3072]{0:T(1024)S(1)} %copy-done.93, bf16[1,256,2048]{2,1,0:T(8,128)(2,1)S(1)} %copy-done, f32[2048]{0:T(1024)S(1)} %copy-done.67, f32[2048]{0:T(1024)S(1)} %copy-done.70, f32[256]{0:T(256)S(1)} %add_rsqrt_fusion, f32[256]{0:T(256)S(1)} %broadcast_multiply_fusion.2), kind=kOutput, calls=%fused_computation.12 | convolution fusion | flops 3225157632 | bytes 16807936 | tf_op jit(solution)/shard_map/dot_general | solution.py:215
  85.4 7.3 %convert_reduce_fusion.5 = (f32[1024]{0:T(1024)}, bf16[256,1024]{1,0:T(8,128)(2,1)}) fusion(f32[256,1024]{1,0:T(8,128)S(1)} %copy-done.94, bf16[4096,2048]{1,0:T(8,128)(2,1)} %param.27, bf16[1,256,2048]{2,1,0:T(8,128)(2,1)S(1)} %copy-done.3, f32[256]{0:T(256)S(1)} %fusion.188), kind=kOutput, calls=%fused_computation.202 | convolution fusion | flops 1094712320 | bytes 6820864 | tf_op jit(solution)/shard_map/rd,fd->rf/dot_general | solution.py:201
  158.5 20.1 %collective-permute-done.6 = bf16[256,2,512]{0,2,1:T(8,128)(2,1)S(1)} collective-permute-done((bf16[256,2,512]{0,2,1:T(8,128)(2,1)S(1)}, bf16[256,2,512]{0,2,1:T(8,128)(2,1)S(1)}, u32[]{:S(2)}, u32[]{:S(2)}) %collective-permute-start.6) | collective-permute-done | bytes 524320 | tf_op jit(solution)/shard_map/ppermute | solution.py:41
  178.7 11.0 %collective-permute-done.28 = bf16[256,2,512]{0,2,1:T(8,128)(2,1)S(1)} collective-permute-done((bf16[256,2,512]{0,2,1:T(8,128)(2,1)S(1)}, bf16[256,2,512]{0,2,1:T(8,128)(2,1)S(1)}, u32[]{:S(2)}, u32[]{:S(2)}) %collective-permute-start.28) | collective-permute-done | bytes 524320 | tf_op jit(solution)/shard_map/ppermute | solution.py:41
  191.5 9.5 %collective-permute-done.40 = bf16[256,1024]{1,0:T(8,128)(2,1)S(1)} collective-permute-done((bf16[256,1024]{1,0:T(8,128)(2,1)}, bf16[256,1024]{1,0:T(8,128)(2,1)S(1)}, u32[]{:S(2)}, u32[]{:S(2)}) %collective-permute-start.40) | collective-permute-done | bytes 524320 | tf_op jit(solution)/shard_map/ppermute | solution.py:41
  203.4 31.0 %collective-permute-done.44 = bf16[256,1024]{1,0:T(8,128)(2,1)S(1)} collective-permute-done((bf16[256,1024]{1,0:T(8,128)(2,1)S(1)}, bf16[256,1024]{1,0:T(8,128)(2,1)S(1)}, u32[]{:S(2)}, u32[]{:S(2)}) %collective-permute-start.44) | collective-permute-done | bytes 524320 | tf_op jit(solution)/shard_map/ppermute | solution.py:41
  270.6 7.4 %collective-permute-done.54 = bf16[1024,256]{1,0:T(8,128)(2,1)S(1)} collective-permute-done((bf16[1024,256]{1,0:T(8,128)(2,1)S(1)}, bf16[1024,256]{1,0:T(8,128)(2,1)S(1)}, u32[]{:S(2)}, u32[]{:S(2)}) %collective-permute-start.54) | collective-permute-done | bytes 524320 | tf_op jit(solution)/shard_map/ppermute | solution.py:41
  281.9 7.4 %collective-permute-done.58 = bf16[1024,256]{1,0:T(8,128)(2,1)S(1)} collective-permute-done((bf16[1024,256]{1,0:T(8,128)(2,1)S(1)}, bf16[1024,256]{1,0:T(8,128)(2,1)S(1)}, u32[]{:S(2)}, u32[]{:S(2)}) %collective-permute-start.58) | collective-permute-done | bytes 524320 | tf_op jit(solution)/shard_map/ppermute | solution.py:41
  293.2 7.3 %collective-permute-done.62 = bf16[1024,256]{1,0:T(8,128)(2,1)S(1)} collective-permute-done((bf16[1024,256]{1,0:T(8,128)(2,1)S(1)}, bf16[1024,256]{1,0:T(8,128)(2,1)S(1)}, u32[]{:S(2)}, u32[]{:S(2)}) %collective-permute-start.62) | collective-permute-done | bytes 524320 | tf_op jit(solution)/shard_map/ppermute | solution.py:41
  304.0 7.7 %collective-permute-done.34 = bf16[256,1024]{1,0:T(8,128)(2,1)S(1)} collective-permute-done((bf16[256,1024]{1,0:T(8,128)(2,1)S(1)}, bf16[256,1024]{1,0:T(8,128)(2,1)S(1)}, u32[]{:S(2)}, u32[]{:S(2)}) %collective-permute-start.34) | collective-permute-done | bytes 524320 | tf_op jit(solution)/shard_map/ppermute | solution.py:41
  316.3 12.3 %collective-permute-done.38 = bf16[256,1024]{1,0:T(8,128)(2,1)S(1)} collective-permute-done((bf16[256,1024]{1,0:T(8,128)(2,1)S(1)}, bf16[256,1024]{1,0:T(8,128)(2,1)S(1)}, u32[]{:S(2)}, u32[]{:S(2)}) %collective-permute-start.38) | collective-permute-done | bytes 524320 | tf_op jit(solution)/shard_map/ppermute | solution.py:41
  332.3 13.1 %collective-permute-done.42 = bf16[256,1024]{1,0:T(8,128)(2,1)S(1)} collective-permute-done((bf16[256,1024]{1,0:T(8,128)(2,1)S(1)}, bf16[256,1024]{1,0:T(8,128)(2,1)S(1)}, u32[]{:S(2)}, u32[]{:S(2)}) %collective-permute-start.42) | collective-permute-done | bytes 524320 | tf_op jit(solution)/shard_map/ppermute | solution.py:41
  348.9 7.1 %collective-permute-done.46 = bf16[256,1024]{1,0:T(8,128)(2,1)S(1)} collective-permute-done((bf16[256,1024]{1,0:T(8,128)(2,1)S(1)}, bf16[256,1024]{1,0:T(8,128)(2,1)S(1)}, u32[]{:S(2)}, u32[]{:S(2)}) %collective-permute-start.46) | collective-permute-done | bytes 524320 | tf_op jit(solution)/shard_map/ppermute | solution.py:41
  364.1 21.9 %collective-permute-done.59 = bf16[1024,128]{1,0:T(8,128)(2,1)S(1)} collective-permute-done((bf16[1024,128]{1,0:T(8,128)(2,1)S(1)}, bf16[1024,128]{1,0:T(8,128)(2,1)S(1)}, u32[]{:S(2)}, u32[]{:S(2)}) %collective-permute-start.59) | collective-permute-done | bytes 262176 | tf_op jit(solution)/shard_map/ppermute | solution.py:41
  386.0 11.2 %collective-permute-done.63 = bf16[1024,128]{1,0:T(8,128)(2,1)S(1)} collective-permute-done((bf16[1024,128]{1,0:T(8,128)(2,1)S(1)}, bf16[1024,128]{1,0:T(8,128)(2,1)S(1)}, u32[]{:S(2)}, u32[]{:S(2)}) %collective-permute-start.63) | collective-permute-done | bytes 262176 | tf_op jit(solution)/shard_map/ppermute | solution.py:41
  397.3 11.2 %collective-permute-done.35 = bf16[128,1024]{1,0:T(8,128)(2,1)S(1)} collective-permute-done((bf16[128,1024]{1,0:T(8,128)(2,1)S(1)}, bf16[128,1024]{1,0:T(8,128)(2,1)S(1)}, u32[]{:S(2)}, u32[]{:S(2)}) %collective-permute-start.35) | collective-permute-done | bytes 262176 | tf_op jit(solution)/shard_map/ppermute | solution.py:41
  420.8 8.5 %collective-permute-done.26 = bf16[256,1024]{0,1:T(8,128)(2,1)S(1)} collective-permute-done((bf16[256,1024]{0,1:T(8,128)(2,1)S(1)}, bf16[256,1024]{0,1:T(8,128)(2,1)S(1)}, u32[]{:S(2)}, u32[]{:S(2)}) %collective-permute-start.26) | collective-permute-done | bytes 524320 | tf_op jit(solution)/shard_map/ppermute | solution.py:41
  451.6 12.3 %collective-permute-done.31 = bf16[1024,128]{1,0:T(8,128)(2,1)S(1)} collective-permute-done((bf16[1024,128]{1,0:T(8,128)(2,1)S(1)}, bf16[1024,128]{1,0:T(8,128)(2,1)S(1)}, u32[]{:S(2)}, u32[]{:S(2)}) %collective-permute-start.31) | collective-permute-done | bytes 262176 | tf_op jit(solution)/shard_map/ppermute | solution.py:41
  478.3 9.7 %fusion.236 = (f32[256]{0:T(256)S(1)}, f32[256]{0:T(256)S(1)}, f32[2048]{0:T(1024)S(1)}, f32[2048]{0:T(1024)S(1)}, f32[2048]{0:T(1024)S(1)}, /*index=5*/f32[2048]{0:T(1024)S(1)}, f32[256,2048]{1,0:T(8,128)S(1)}) fusion(f32[256]{0:T(256)S(1)} %copy-done.62, f32[256]{0:T(256)S(1)} %copy-done.54, bf16[1,256,2048]{2,1,0:T(8,128)(2,1)S(1)} %copy-done.1, ...), kind=kOutput, calls=%fused_computation.457 | convolution fusion | flops 3229081088 | bytes 19451904 | tf_op jit(solution)/shard_map/rc,dc->rd/dot_general | solution.py:290
  498.3 59.7 %psum.49 = f32[4,2048]{1,0:T(4,128)S(1)} all-reduce(f32[4,2048]{1,0:T(4,128)S(1)} %pad_maximum_fusion.68), channel_id=1, replica_groups=mesh['dp'=4,'ctx'=4,'tensor'=2] {'dp','ctx','tensor'}, use_global_device_ids=true, to_apply=%region_12.13 | all-reduce | flops 8192 | bytes 65536 | tf_op jit(solution)/shard_map/psum | solution.py:310
  568.9 12.4 %all-reduce = (f32[3072]{0:T(1024)S(1)}, f32[2048]{0:T(1024)S(1)}, f32[4096]{0:T(1024)S(1)}) all-reduce(f32[3072]{0:T(1024)S(1)} %reduce_sum.167, f32[2048]{0:T(1024)S(1)} %get-tuple-element.43, f32[4096]{0:T(1024)S(1)} %pad_maximum_fusion.69), channel_id=1, replica_groups=mesh['dp'=4,'ctx'=4,'tensor'=2] {'ctx'}, use_global_device_ids=true, to_apply=%region_14.15 | all-reduce | flops 9216 | bytes 73728 | tf_op jit(solution)/shard_map/psum | solution.py:314
  581.3 19.1 %all-reduce.1 = (f32[3072]{0:T(1024)}, f32[2048]{0:T(1024)S(1)}, f32[4096]{0:T(1024)}) all-reduce(f32[3072]{0:T(1024)S(1)} %get-tuple-element.24, f32[2048]{0:T(1024)S(1)} %get-tuple-element.25, f32[4096]{0:T(1024)S(1)} %get-tuple-element.26), channel_id=1, replica_groups=mesh['dp'=4,'ctx'=4,'tensor'=2] {'dp'}, use_global_device_ids=true, to_apply=%region_15.16 | all-reduce | flops 9216 | bytes 73728 | tf_op jit(solution)/shard_map/psum | solution.py:314
  620.9 8.8 %collective-permute-done.16 = bf16[256,768]{1,0:T(8,128)(2,1)S(1)} collective-permute-done((bf16[256,768]{1,0:T(8,128)(2,1)S(1)}, bf16[256,768]{1,0:T(8,128)(2,1)S(1)}, u32[]{:S(2)}, u32[]{:S(2)}) %collective-permute-start.16) | collective-permute-done | bytes 393248 | tf_op jit(solution)/shard_map/ppermute | solution.py:41
  631.6 8.3 %collective-permute-done.20 = bf16[256,768]{1,0:T(8,128)(2,1)S(1)} collective-permute-done((bf16[256,768]{1,0:T(8,128)(2,1)S(1)}, bf16[256,768]{1,0:T(8,128)(2,1)S(1)}, u32[]{:S(2)}, u32[]{:S(2)}) %collective-permute-start.20) | collective-permute-done | bytes 393248 | tf_op jit(solution)/shard_map/ppermute | solution.py:41
  (546 shorter events, 322.2 us)
Async XLA Ops:
  11.1 131.1 %collective-permute-start.48 = (bf16[256,1024]{1,0:T(8,128)(2,1)}, bf16[256,1024]{1,0:T(8,128)(2,1)}, u32[]{:S(2)}, u32[]{:S(2)}) collective-permute-start(bf16[256,1024]{1,0:T(8,128)(2,1)} %get-tuple-element.111), channel_id=1, source_target_pairs={{0,4},{2,6},{4,0},{6,2},{1,5},{3,7},{5,1},{7,3},{8,12},{10,14},{12... | collective-permute-start | bytes 1572872 | tf_op jit(solution)/shard_map/ppermute | solution.py:41
  18.7 127.8 %collective-permute-start.52 = (bf16[256,1024]{1,0:T(8,128)(2,1)}, bf16[256,1024]{1,0:T(8,128)(2,1)}, u32[]{:S(2)}, u32[]{:S(2)}) collective-permute-start(bf16[256,1024]{1,0:T(8,128)(2,1)} %get-tuple-element.109), channel_id=1, source_target_pairs={{0,4},{2,6},{4,0},{6,2},{1,5},{3,7},{5,1},{7,3},{8,12},{10,14},{12... | collective-permute-start | bytes 1572872 | tf_op jit(solution)/shard_map/ppermute | solution.py:41
  23.3 125.5 %collective-permute-start.56 = (bf16[256,1024]{1,0:T(8,128)(2,1)}, bf16[256,1024]{1,0:T(8,128)(2,1)}, u32[]{:S(2)}, u32[]{:S(2)}) collective-permute-start(bf16[256,1024]{1,0:T(8,128)(2,1)} %get-tuple-element.113), channel_id=1, source_target_pairs={{0,4},{2,6},{4,0},{6,2},{1,5},{3,7},{5,1},{7,3},{8,12},{10,14},{12... | collective-permute-start | bytes 1572872 | tf_op jit(solution)/shard_map/ppermute | solution.py:41
  30.1 122.9 %collective-permute-start.60 = (bf16[256,1024]{1,0:T(8,128)(2,1)}, bf16[256,1024]{1,0:T(8,128)(2,1)}, u32[]{:S(2)}, u32[]{:S(2)}) collective-permute-start(bf16[256,1024]{1,0:T(8,128)(2,1)} %get-tuple-element.115), channel_id=1, source_target_pairs={{0,4},{2,6},{4,0},{6,2},{1,5},{3,7},{5,1},{7,3},{8,12},{10,14},{12... | collective-permute-start | bytes 1572872 | tf_op jit(solution)/shard_map/ppermute | solution.py:41
  30.7 107.6 %collective-permute-start.8 = (f32[1,2,256]{2,1,0:T(2,128)}, f32[1,2,256]{2,1,0:T(2,128)}, u32[]{:S(2)}, u32[]{:S(2)}) collective-permute-start(f32[1,2,256]{2,1,0:T(2,128)} %maximum_bitcast_fusion.9), channel_id=1, source_target_pairs={{0,4},{2,6},{4,0},{6,2},{1,5},{3,7},{5,1},{7,3},{8,12},{10,14},{12... | collective-permute-start | bytes 6152 | tf_op jit(solution)/shard_map/ppermute | solution.py:41
  142.2 47.6 %collective-permute-start.36 = (bf16[256,1024]{1,0:T(8,128)(2,1)}, bf16[256,1024]{1,0:T(8,128)(2,1)S(1)}, u32[]{:S(2)}, u32[]{:S(2)}) collective-permute-start(bf16[256,1024]{1,0:T(8,128)(2,1)} %get-tuple-element.122), channel_id=1, source_target_pairs={{0,4},{2,6},{4,0},{6,2},{1,5},{3,7},{5,1},{7,3},{8,12},{10,14},{12... | collective-permute-start | bytes 1572872 | tf_op jit(solution)/shard_map/ppermute | solution.py:41
  153.1 48.0 %collective-permute-start.40 = (bf16[256,1024]{1,0:T(8,128)(2,1)}, bf16[256,1024]{1,0:T(8,128)(2,1)S(1)}, u32[]{:S(2)}, u32[]{:S(2)}) collective-permute-start(bf16[256,1024]{1,0:T(8,128)(2,1)} %get-tuple-element.120), channel_id=1, source_target_pairs={{0,4},{2,6},{4,0},{6,2},{1,5},{3,7},{5,1},{7,3},{8,12},{10,14},{12... | collective-permute-start | bytes 1572872 | tf_op jit(solution)/shard_map/ppermute | solution.py:41
  156.1 81.7 %collective-permute-start = (bf16[256,2,1024]{0,2,1:T(8,128)(2,1)S(1)}, bf16[256,2,1024]{0,2,1:T(8,128)(2,1)S(1)}, u32[]{:S(2)}, u32[]{:S(2)}) collective-permute-start(bf16[256,2,1024]{0,2,1:T(8,128)(2,1)S(1)} %maximum_bitcast_fusion.1), channel_id=1, source_target_pairs={{0,4},{2,6},{4,0},{6,2},{1,5},{3,7},{5,1},{7,3},{8,12},{10,14},{12... | collective-permute-start | bytes 3145736 | tf_op jit(solution)/shard_map/ppermute | solution.py:41
  178.6 55.8 %collective-permute-start.44 = (bf16[256,1024]{1,0:T(8,128)(2,1)S(1)}, bf16[256,1024]{1,0:T(8,128)(2,1)S(1)}, u32[]{:S(2)}, u32[]{:S(2)}) collective-permute-start(bf16[256,1024]{1,0:T(8,128)(2,1)S(1)} %get-tuple-element.118), channel_id=1, source_target_pairs={{0,4},{2,6},{4,0},{6,2},{1,5},{3,7},{5,1},{7,3},{8,12},{10,14},{12... | collective-permute-start | bytes 1572872 | tf_op jit(solution)/shard_map/ppermute | solution.py:41
  189.8 51.6 %collective-permute-start.49 = (bf16[512,1024]{1,0:T(8,128)(2,1)}, bf16[512,1024]{1,0:T(8,128)(2,1)}, u32[]{:S(2)}, u32[]{:S(2)}) collective-permute-start(bf16[512,1024]{1,0:T(8,128)(2,1)} %pad_maximum_fusion.26), channel_id=1, source_target_pairs={{0,2},{2,0},{4,6},{6,4},{1,3},{3,1},{5,7},{7,5},{8,10},{10,8},{12,... | collective-permute-start | bytes 3145736 | tf_op jit(solution)/shard_map/ppermute | solution.py:41
  189.8 45.7 %collective-permute-start.7 = (bf16[512,1,512]{0,2,1:T(8,128)(2,1)S(1)}, bf16[512,1,512]{0,2,1:T(8,128)(2,1)S(1)}, u32[]{:S(2)}, u32[]{:S(2)}) collective-permute-start(bf16[512,1,512]{0,2,1:T(8,128)(2,1)S(1)} %get-tuple-element.54), channel_id=1, source_target_pairs={{0,2},{2,0},{4,6},{6,4},{1,3},{3,1},{5,7},{7,5},{8,10},{10,8},{12,... | collective-permute-start | bytes 1572872 | tf_op jit(solution)/shard_map/ppermute | solution.py:41
  249.4 159.1 %collective-permute-start.1 = (bf16[512,2,1024]{0,2,1:T(8,128)(2,1)S(1)}, bf16[512,2,1024]{0,2,1:T(8,128)(2,1)S(1)}, u32[]{:S(2)}, u32[]{:S(2)}) collective-permute-start(bf16[512,2,1024]{0,2,1:T(8,128)(2,1)S(1)} %copy-done.12), channel_id=1, source_target_pairs={{0,2},{2,0},{4,6},{6,4},{1,3},{3,1},{5,7},{7,5},{8,10},{10,8},{12,... | collective-permute-start | bytes 6291464 | tf_op jit(solution)/shard_map/ppermute | solution.py:41
  278.0 50.6 %collective-permute-start.38 = (bf16[256,1024]{1,0:T(8,128)(2,1)S(1)}, bf16[256,1024]{1,0:T(8,128)(2,1)S(1)}, u32[]{:S(2)}, u32[]{:S(2)}) collective-permute-start(bf16[256,1024]{1,0:T(8,128)(2,1)S(1)} %convolution_convert_fusion.6), channel_id=1, source_target_pairs={{0,8},{8,0},{16,24},{24,16},{1,9},{9,1},{17,25},{25,17},{2,10},{10... | collective-permute-start | bytes 1572872 | tf_op jit(solution)/shard_map/ppermute | solution.py:41
  289.3 56.2 %collective-permute-start.42 = (bf16[256,1024]{1,0:T(8,128)(2,1)S(1)}, bf16[256,1024]{1,0:T(8,128)(2,1)S(1)}, u32[]{:S(2)}, u32[]{:S(2)}) collective-permute-start(bf16[256,1024]{1,0:T(8,128)(2,1)S(1)} %convolution_convert_fusion.5), channel_id=1, source_target_pairs={{0,8},{8,0},{16,24},{24,16},{1,9},{9,1},{17,25},{25,17},{2,10},{10... | collective-permute-start | bytes 1572872 | tf_op jit(solution)/shard_map/ppermute | solution.py:41
  300.5 55.5 %collective-permute-start.46 = (bf16[256,1024]{1,0:T(8,128)(2,1)S(1)}, bf16[256,1024]{1,0:T(8,128)(2,1)S(1)}, u32[]{:S(2)}, u32[]{:S(2)}) collective-permute-start(bf16[256,1024]{1,0:T(8,128)(2,1)S(1)} %convolution_convert_fusion.4), channel_id=1, source_target_pairs={{0,8},{8,0},{16,24},{24,16},{1,9},{9,1},{17,25},{25,17},{2,10},{10... | collective-permute-start | bytes 1572872 | tf_op jit(solution)/shard_map/ppermute | solution.py:41
  311.7 48.8 %collective-permute-start.51 = (bf16[1024,128]{1,0:T(8,128)(2,1)S(1)}, bf16[1024,128]{1,0:T(8,128)(2,1)S(1)}, u32[]{:S(2)}, u32[]{:S(2)}) collective-permute-start(bf16[1024,128]{1,0:T(8,128)(2,1)S(1)} %slice.843), channel_id=1, source_target_pairs={{0,16},{8,24},{16,0},{24,8},{1,17},{9,25},{17,1},{25,9},{2,18},{10... | collective-permute-start | bytes 786440 | tf_op jit(solution)/shard_map/ppermute | solution.py:41
  360.5 47.9 %collective-permute-start.35 = (bf16[128,1024]{1,0:T(8,128)(2,1)S(1)}, bf16[128,1024]{1,0:T(8,128)(2,1)S(1)}, u32[]{:S(2)}, u32[]{:S(2)}) collective-permute-start(bf16[128,1024]{1,0:T(8,128)(2,1)S(1)} %slice.847), channel_id=1, source_target_pairs={{0,16},{8,24},{16,0},{24,8},{1,17},{9,25},{17,1},{25,9},{2,18},{10... | collective-permute-start | bytes 786440 | tf_op jit(solution)/shard_map/ppermute | solution.py:41
  362.4 56.0 %collective-permute-start.39 = (bf16[128,1024]{1,0:T(8,128)(2,1)}, bf16[128,1024]{1,0:T(8,128)(2,1)}, u32[]{:S(2)}, u32[]{:S(2)}) collective-permute-start(bf16[128,1024]{1,0:T(8,128)(2,1)} %slice.846), channel_id=1, source_target_pairs={{0,16},{8,24},{16,0},{24,8},{1,17},{9,25},{17,1},{25,9},{2,18},{10... | collective-permute-start | bytes 786440 | tf_op jit(solution)/shard_map/ppermute | solution.py:41
  441.2 48.2 %collective-permute-start.2 = (bf16[256,2048]{1,0:T(8,128)(2,1)}, bf16[256,2048]{1,0:T(8,128)(2,1)}, u32[]{:S(2)}, u32[]{:S(2)}) collective-permute-start(bf16[256,2048]{1,0:T(8,128)(2,1)} %fusion.57), channel_id=1, source_target_pairs={{0,1},{1,0},{2,3},{3,2},{4,5},{5,4},{6,7},{7,6},{8,9},{9,8},{10,11... | collective-permute-start | bytes 3145736 | tf_op jit(solution)/shard_map/ppermute | solution.py:41
  489.0 69.0 %collective-permute-start.10 = (bf16[256,768]{0,1:T(8,128)(2,1)}, bf16[256,768]{0,1:T(8,128)(2,1)}, u32[]{:S(2)}, u32[]{:S(2)}) collective-permute-start(bf16[256,768]{0,1:T(8,128)(2,1)} %get-tuple-element.37), channel_id=1, source_target_pairs={{0,4},{2,6},{4,0},{6,2},{1,5},{3,7},{5,1},{7,3},{8,12},{10,14},{12... | collective-permute-start | bytes 1179656 | tf_op jit(solution)/shard_map/ppermute | solution.py:41
  493.1 73.0 %collective-permute-start.5 = (bf16[256,2048]{1,0:T(8,128)(2,1)S(1)}, bf16[256,2048]{1,0:T(8,128)(2,1)}, u32[]{:S(2)}, u32[]{:S(2)}) collective-permute-start(bf16[256,2048]{1,0:T(8,128)(2,1)S(1)} %get-tuple-element.61), channel_id=1, source_target_pairs={{0,1},{1,0},{2,3},{3,2},{4,5},{5,4},{6,7},{7,6},{8,9},{9,8},{10,11... | collective-permute-start | bytes 3145736 | tf_op jit(solution)/shard_map/ppermute | solution.py:41
  494.7 66.1 %collective-permute-start.14 = (bf16[256,768]{0,1:T(8,128)(2,1)}, bf16[256,768]{0,1:T(8,128)(2,1)S(1)}, u32[]{:S(2)}, u32[]{:S(2)}) collective-permute-start(bf16[256,768]{0,1:T(8,128)(2,1)} %get-tuple-element.40), channel_id=1, source_target_pairs={{0,4},{2,6},{4,0},{6,2},{1,5},{3,7},{5,1},{7,3},{8,12},{10,14},{12... | collective-permute-start | bytes 1179656 | tf_op jit(solution)/shard_map/ppermute | solution.py:41
  496.2 67.3 %collective-permute-start.18 = (bf16[256,768]{0,1:T(8,128)(2,1)S(1)}, bf16[256,768]{0,1:T(8,128)(2,1)S(1)}, u32[]{:S(2)}, u32[]{:S(2)}) collective-permute-start(bf16[256,768]{0,1:T(8,128)(2,1)S(1)} %get-tuple-element.39), channel_id=1, source_target_pairs={{0,4},{2,6},{4,0},{6,2},{1,5},{3,7},{5,1},{7,3},{8,12},{10,14},{12... | collective-permute-start | bytes 1179656 | tf_op jit(solution)/shard_map/ppermute | solution.py:41
  496.7 67.8 %collective-permute-start.22 = (bf16[256,768]{0,1:T(8,128)(2,1)S(1)}, bf16[256,768]{0,1:T(8,128)(2,1)S(1)}, u32[]{:S(2)}, u32[]{:S(2)}) collective-permute-start(bf16[256,768]{0,1:T(8,128)(2,1)S(1)} %get-tuple-element.38), channel_id=1, source_target_pairs={{0,4},{2,6},{4,0},{6,2},{1,5},{3,7},{5,1},{7,3},{8,12},{10,14},{12... | collective-permute-start | bytes 1179656 | tf_op jit(solution)/shard_map/ppermute | solution.py:41
  (154 other events, 1969.1 us)
